TPU v7x, 32 devices: a whole 2x2x4 slice. The times are simulated.
32 devices in a mesh: grp: 2 (over y), row: 4 (over x, core), col: 4 (over z).
Axes of the slice: x: 2, y: 2, z: 4, core: 2. Of those that a mesh axis runs over, the one named last changes fastest.
Arguments:
- left_factors: bfloat16 [8, 48, 32, 128], P(('grp', 'row'), 'col'), parts along dimension 0, may hold values from -6 to 6
- right_factors: bfloat16 [8, 48, 32, 128], P(('grp', 'col'), 'row'), parts along dimension 0, may hold values from -6 to 6
- out_weight: bfloat16 [1024, 128], replicated, may hold values from -2 to 2
- out_bias: float32 [128], replicated, may hold values from -4 to 4
- pair_grad: bfloat16 [384, 192, 128], P(('grp', 'row'), 'col'), parts along dimension 0, may hold values from -6 to 6
Outputs:
- pair_update: bfloat16 [384, 192, 128], P(('grp', 'row'), 'col'), parts along dimension 0
- grad_left: float32 [8, 48, 32, 128], P(('grp', 'row'), 'col'), parts along dimension 0
- grad_right: float32 [8, 48, 32, 128], P(('grp', 'col'), 'row'), parts along dimension 0
- grad_weight: float32 [2048, 128], P('grp'), parts along dimension 0
There are 2 independent parts, one for each index of `grp`. A program takes and returns all parts, laid end to end along the dimension named above; an argument that names none is the same for every part. Nothing has to cross between parts.
All inputs are finite; a program needn't handle non-finite values.
Results may differ from a plain program's by a relative error of at most 0.004.
Values may be sent and summed in bfloat16 or wider, within the bound.
A program may use at most 64 MiB of HBM per device.

v0:
```python
import functools

import jax
import jax.numpy as jnp
from jax import lax
from jax.experimental import pallas as pl
from jax.experimental.pallas import tpu as pltpu
from jax.sharding import PartitionSpec as P

BF = jnp.bfloat16
F32 = jnp.float32
MESH = pl.DeviceIdType.MESH
VMEM = pl.BlockSpec(memory_space=pltpu.VMEM)
HBM = pl.BlockSpec(memory_space=pltpu.HBM)


def greet(n_row, n_col, row, col):
    barrier = pltpu.get_barrier_semaphore()
    for d in range(1, n_row):
        pl.semaphore_signal(barrier, inc=1, device_id={"row": lax.rem(row + d, n_row)}, device_id_type=MESH)
    for d in range(1, n_col):
        pl.semaphore_signal(barrier, inc=1, device_id={"col": lax.rem(col + d, n_col)}, device_id_type=MESH)
    pl.semaphore_wait(barrier, n_row + n_col - 2)


def spread(src_of, dst, axis, n, me, send, recv):
    copies = []
    for d in range(1, n):
        to = lax.rem(me + d, n)
        copy = pltpu.make_async_remote_copy(
            src_ref=src_of(to), dst_ref=dst, send_sem=send.at[d - 1], recv_sem=recv.at[d - 1],
            device_id={axis: to}, device_id_type=MESH,
        )
        copy.start()
        copies.append(copy)
    return copies


def send_parts(src_of, slots, axis, n, me, send, recv):
    copies = []
    for d in range(1, n):
        to = lax.rem(me + d, n)
        copy = pltpu.make_async_remote_copy(
            src_ref=src_of(to), dst_ref=slots.at[d - 1], send_sem=send.at[d - 1], recv_sem=recv.at[d - 1],
            device_id={axis: to}, device_id_type=MESH,
        )
        copy.start()
        copies.append(copy)
    return copies


def nn(a, b):
    return lax.dot_general(a, b, (((1,), (0,)), ((), ())), preferred_element_type=F32)


def nt(a, b):
    return lax.dot_general(a, b, (((1,), (1,)), ((), ())), preferred_element_type=F32)


def twice(body):
    def pair_of(p):
        body(p * 2)
        body(p * 2 + 1)

    return pair_of


def whole_kernel(
    n_row, n_col, inv_s, inv_w,
    left_h, right_h, weight_h, bias_h, grad_h,
    out_p, out_l, out_r, out_w,
    pair, sum_l, sum_r, left, right, weight, bias, grad,
    f_rows, f_w, a2, a2t, b2t, wp, wpt, xs, gs, gw_acc, gl_acc, gr_t,
    gl, gr, gw, l_in, r_in, w_in, w_col, w_col_in, w_own, w_half,
    ls, lr, rs, rr, gls, glr, grs, grr, ws, wr, vs, vr, us, ur, ts, tr, loc,
):
    row, col = lax.axis_index("row"), lax.axis_index("col")
    loads = [
        pltpu.make_async_copy(src, dst, loc.at[at])
        for at, (src, dst) in enumerate((
            (weight_h, weight), (grad_h, grad), (bias_h, bias),
            (right_h, right.at[row]), (left_h, left.at[col]),
        ))
    ]
    for copy in loads:
        copy.start()
    _, piece_l, n_c, n_s = left.shape
    _, piece_r, n_e, _ = right.shape
    n_i, n_j = n_col * piece_l, n_row * piece_r
    n_h = weight.shape[1]
    half = n_i // 2
    pad = 64
    lanes = 2 * pad
    greet(n_row, n_col, row, col)
    c_left = spread(lambda to: left_h, left.at[col], "col", n_col, col, ls, lr)
    c_right = spread(lambda to: right_h, right.at[row], "row", n_row, row, rs, rr)

    loads[0].wait()
    f_w[...] = weight[...].astype(F32).reshape(n_c, n_e, n_h)
    for e in range(n_e):
        wp[e * n_c : (e + 1) * n_c, :] = f_w[:, e, :].astype(BF)
    wpt[...] = wp[...].T
    loads[1].wait()
    loads[2].wait()
    zeros = jnp.zeros((pad - n_j, n_h), BF)

    def grads(ip, count):
        rows = []
        for q in range(count):
            rows += [grad[ip + q], zeros, grad[half + ip + q], zeros]
        return jnp.concatenate(rows, axis=0)

    @pl.loop(0, half // 2)
    def _(p):
        ip = p * 2
        og = nt(wp[...], grads(ip, 2)).astype(BF)
        for q in range(2):
            gs[ip + q] = og[:, q * lanes : (q + 1) * lanes].reshape(n_e, n_c, lanes)

    b2t[...] = jnp.zeros_like(b2t)
    loads[3].wait()
    for copy in c_right:
        copy.wait()
    f_rows[...] = right[...].reshape(n_j, n_e, n_s).astype(F32)
    for e in range(n_e):
        block = f_rows[:, e, :].astype(BF)
        b2t[e, 0:n_j, 0:n_s] = block
        b2t[e, pad : pad + n_j, n_s : 2 * n_s] = block

    gl_acc[...] = jnp.zeros_like(gl_acc)

    @pl.loop(0, n_e // 4)
    def _(p):
        e = p * 4
        g = jnp.concatenate([gs[:, e + q].reshape(half * n_c, lanes) for q in range(4)], axis=1)
        gl_acc[...] += nn(g, b2t[pl.ds(e, 4)].reshape(4 * lanes, 2 * n_s))

    for ii in range(2):
        gl[ii * half : (ii + 1) * half] = gl_acc[:, ii * n_s : (ii + 1) * n_s].reshape(half, n_c, n_s).astype(BF)
    loads[4].wait()
    for copy in c_left:
        copy.wait()
    flat = left[...].reshape(n_i, n_c, n_s)
    for ii in range(2):
        a2[:, ii * n_s : (ii + 1) * n_s] = flat[ii * half : (ii + 1) * half].reshape(half * n_c, n_s)
    c_l = send_parts(lambda to: gl.at[pl.ds(to * piece_l, piece_l)], l_in, "col", n_col, col, gls, glr)

    width = n_e // 2
    rows = width * n_c

    def means(ip, count, first, size):
        return jnp.concatenate(
            [xs[ip + q, first : first + size].reshape(size * n_c, lanes) for q in range(count)], axis=1
        )

    def terms(hf):
        first = hf * width

        def mean(p):
            e = first + p * 2
            out = nt(a2[...], b2t[pl.ds(e, 2)].reshape(2 * lanes, 2 * n_s)).astype(BF)
            for q in range(2):
                xs[:, pl.ds(e + q, 1)] = out[:, q * lanes : (q + 1) * lanes].reshape(half, 1, n_c, lanes)

        pl.loop(0, width // 4)(twice(mean))
        gw_acc[...] = jnp.zeros_like(gw_acc)

        @pl.loop(0, half // 4)
        def _(p):
            gw_acc[...] += nn(means(p * 4, 4, first, width), grads(p * 4, 4))

        gw[hf] = gw_acc[...].reshape(gw.shape[1:]).astype(BF)

    def phase_1(hf):
        return send_parts(lambda to: gw.at[hf, to], w_in.at[hf], "row", n_row, row, ws.at[hf], wr.at[hf])

    def sum_1(hf, copies):
        for copy in copies:
            copy.wait()
        total = gw[hf, row].astype(F32)
        for d in range(n_row - 1):
            total += w_in[hf, d].astype(F32)
        w_col[hf] = total.reshape(w_col.shape[1:]).astype(BF)

    def phase_2(hf):
        return send_parts(lambda to: w_col.at[hf, to], w_col_in.at[hf], "col", n_col, col, vs.at[hf], vr.at[hf])

    def sum_2(hf, copies):
        for copy in copies:
            copy.wait()
        total = w_col[hf, col].astype(F32)
        for d in range(n_col - 1):
            total += w_col_in[hf, d].astype(F32)
        w_own[hf] = (total * inv_w).astype(BF)

    def phase_3(hf):
        mine = pltpu.make_async_copy(w_own.at[hf], w_half.at[hf, col], loc.at[5 + hf])
        mine.start()
        return [mine] + spread(
            lambda to: w_own.at[hf], w_half.at[hf, col], "col", n_col, col, us.at[hf], ur.at[hf]
        )

    def phase_4(hf, copies):
        for copy in copies:
            copy.wait()
        mine = pltpu.make_async_copy(w_half.at[hf], out_w.at[hf, row], loc.at[7 + hf])
        mine.start()
        return [mine] + spread(
            lambda to: w_half.at[hf], out_w.at[hf, row], "row", n_row, row, ts.at[hf], tr.at[hf]
        )

    lane = lax.broadcasted_iota(jnp.int32, (n_s, lanes), 1)

    def rights(p):
        e = p * 2
        g = jnp.concatenate([gs[:, e + q].reshape(half * n_c, lanes) for q in range(2)], axis=1)
        t = nn(a2t[...], g)
        for q in range(2):
            z = jnp.where(
                lane < pad,
                t[0:n_s, q * lanes : (q + 1) * lanes],
                t[n_s : 2 * n_s, q * lanes : (q + 1) * lanes],
            ).T
            gr_t[e + q] = z[0:n_j] + z[pad : pad + n_j]

    def update(p):
        ip = p * 2
        up = nn(wpt[...], means(ip, 2, 0, n_e))
        for q in range(2):
            u = (up[:, q * lanes : (q + 1) * lanes].T * inv_s + bias[...]).astype(BF)
            pair[ip + q] = u[0:n_j]
            pair[half + ip + q] = u[pad : pad + n_j]

    terms(0)
    a2t[...] = a2[...].T
    w_a = phase_1(0)
    terms(1)
    sum_1(0, w_a)
    w_b = phase_1(1)
    w_a = phase_2(0)
    pl.loop(0, width // 4)(twice(rights))
    sum_1(1, w_b)
    sum_2(0, w_a)
    w_b = phase_2(1)
    w_a = phase_3(0)
    pl.loop(width // 4, width // 2)(twice(rights))
    for e in range(n_e):
        f_rows[:, e, :] = gr_t[e]
    gr[...] = f_rows[...].astype(BF)
    sum_2(1, w_b)
    w_a = phase_4(0, w_a)
    w_b = phase_3(1)
    c_r = send_parts(lambda to: gr.at[pl.ds(to * piece_r, piece_r)], r_in, "row", n_row, row, grs, grr)
    early = half // 4 - half // 12
    pl.loop(0, early)(twice(update))
    w_b = phase_4(1, w_b)
    pl.loop(early, half // 4)(twice(update))
    gives = [pltpu.make_async_copy(pair, out_p, loc.at[9])]
    gives[0].start()
    for copy in c_l:
        copy.wait()
    total = gl[pl.ds(col * piece_l, piece_l)].astype(F32)
    for d in range(n_col - 1):
        total += l_in[d].astype(F32)
    sum_l[0] = total * inv_s
    gives.append(pltpu.make_async_copy(sum_l, out_l, loc.at[10]))
    gives[1].start()
    for copy in c_r:
        copy.wait()
    total = gr[pl.ds(row * piece_r, piece_r)].astype(F32)
    for d in range(n_row - 1):
        total += r_in[d].astype(F32)
    sum_r[0] = total * inv_s
    gives.append(pltpu.make_async_copy(sum_r, out_r, loc.at[11]))
    gives[2].start()
    for copy in w_a + w_b + gives:
        copy.wait()


def tail_kernel(*refs):
    inner, outer, held = refs[:4], refs[4:8], refs[8:12]
    wide, mixed, arrived, left = refs[12:]
    takes = [pltpu.make_async_copy(inner[at], held[at], arrived.at[at]) for at in range(4)]
    gives = [
        pltpu.make_async_copy(wide if at == 3 else held[at], outer[at], left.at[at]) for at in range(4)
    ]
    for at in (3, 0, 1, 2):
        takes[at].start()
    for at in (3, 0, 1, 2):
        takes[at].wait()
        if at == 3:
            n_c, n_e, _ = mixed.shape
            flat = held[3][...].astype(F32).reshape(wide.shape)
            for e in range(n_e):
                mixed[:, e, :] = flat[e * n_c : (e + 1) * n_c]
            wide[...] = mixed[...].reshape(wide.shape)
        gives[at].start()
    for copy in gives:
        copy.wait()


def dma(n):
    return pltpu.SemaphoreType.DMA((max(n, 1),))


def dma2(n):
    return pltpu.SemaphoreType.DMA((2, n))


def on_device(n_row, n_col, left, right, weight, bias, grad):
    _, piece_l, n_c, n_s = left.shape
    _, piece_r, n_e, _ = right.shape
    n_k, n_h = weight.shape
    n_i, n_j = piece_l * n_col, piece_r * n_row
    half, lanes = n_i // 2, 128
    part = n_k // 2 // n_row
    small = part // n_col
    shapes = (
        jax.ShapeDtypeStruct((n_i, n_j, n_h), BF),
        jax.ShapeDtypeStruct((1, piece_l, n_c, n_s), F32),
        jax.ShapeDtypeStruct((1, piece_r, n_e, n_s), F32),
        jax.ShapeDtypeStruct((n_k, n_h), F32),
    )
    held = shapes[:3] + (jax.ShapeDtypeStruct((2, n_row, n_col, small, n_h), BF),)
    results = pl.pallas_call(
        functools.partial(whole_kernel, n_row, n_col, 1.0 / n_s, 1.0 / (n_s * n_i * n_row)),
        out_shape=held,
        in_specs=[HBM] * 5,
        out_specs=(HBM,) * 4,
        scratch_shapes=[pltpu.VMEM(shape.shape, shape.dtype) for shape in held[:3]]
        + [
            pltpu.VMEM((n_col, piece_l, n_c, n_s), BF),
            pltpu.VMEM((n_row, piece_r, n_e, n_s), BF),
            pltpu.VMEM((n_k, n_h), BF),
            pltpu.VMEM((1, n_h), F32),
            pltpu.VMEM((n_i, n_j, n_h), BF),
            pltpu.VMEM((n_j, n_e, n_s), F32),
            pltpu.VMEM((n_c, n_e, n_h), F32),
            pltpu.VMEM((half * n_c, 2 * n_s), BF),
            pltpu.VMEM((2 * n_s, half * n_c), BF),
            pltpu.VMEM((n_e, lanes, 2 * n_s), BF),
            pltpu.VMEM((n_k, n_h), BF),
            pltpu.VMEM((n_h, n_k), BF),
            pltpu.VMEM((half, n_e, n_c, lanes), BF),
            pltpu.VMEM((half, n_e, n_c, lanes), BF),
            pltpu.VMEM((n_k // 2, n_h), F32),
            pltpu.VMEM((half * n_c, 2 * n_s), F32),
            pltpu.VMEM((n_e, n_j, n_s), F32),
            pltpu.VMEM((n_i, n_c, n_s), BF),
            pltpu.VMEM((n_j, n_e, n_s), BF),
            pltpu.VMEM((2, n_row, part, n_h), BF),
            pltpu.VMEM((n_col - 1, piece_l, n_c, n_s), BF),
            pltpu.VMEM((n_row - 1, piece_r, n_e, n_s), BF),
            pltpu.VMEM((2, n_row - 1, part, n_h), BF),
            pltpu.VMEM((2, n_col, small, n_h), BF),
            pltpu.VMEM((2, n_col - 1, small, n_h), BF),
            pltpu.VMEM((2, small, n_h), BF),
            pltpu.VMEM((2, n_col, small, n_h), BF),
        ]
        + [dma(n_col)] * 2
        + [dma(n_row)] * 2
        + [dma(n_col)] * 2
        + [dma(n_row)] * 2
        + [dma2(n_row)] * 2
        + [dma2(n_col)] * 4
        + [dma2(n_row)] * 2
        + [dma(12)],
        compiler_params=pltpu.CompilerParams(
            collective_id=0, has_side_effects=True, vmem_limit_bytes=67043328 - 1536 * 1024
        ),
        name="whole",
    )(left[0], right[0], weight, bias.reshape(1, n_h), grad)
    return pl.pallas_call(
        tail_kernel,
        out_shape=shapes,
        in_specs=[HBM] * 4,
        out_specs=(HBM,) * 4,
        scratch_shapes=[pltpu.VMEM(shape.shape, shape.dtype) for shape in held + shapes[3:]]
        + [pltpu.VMEM((n_c, n_e, n_h), F32)]
        + [dma(4), dma(4)],
        name="tail",
    )(*results)


def solution(mesh):
    return jax.shard_map(
        functools.partial(on_device, mesh.shape["row"], mesh.shape["col"]),
        mesh=mesh,
        in_specs=(
            P(("grp", "row"), "col", None, None),
            P(("grp", "col"), "row", None, None),
            P(),
            P(),
            P(("grp", "row"), "col", None),
        ),
        out_specs=(
            P(("grp", "row"), "col", None),
            P(("grp", "row"), "col", None, None),
            P(("grp", "col"), "row", None, None),
            P("grp", None),
        ),
        check_vma=False,
    )
```

profile of v0, /device:TPU:0, one launch (start us, length us, event | category | flops | bytes accessed | tf_op | source)
XLA Modules:
  0.0 42.0 jit_solution(18025234068316909637)
XLA Ops:
  0.6 38.7 %whole.1 = (bf16[48,48,128]{2,1,0:T(8,128)(2,1)}, f32[1,12,32,128]{3,2,1,0:T(8,128)}, f32[1,12,32,128]{3,2,1,0:T(8,128)}, bf16[2,4,4,32,128]{4,3,2,1,0:T(8,128)(2,1)}) custom-call(bf16[12,32,128]{2,1,0:T(8,128)(2,1)} %bitcast.3, bf16[12,32,128]{2,1,0:T(8,128)(2,1)} %bitcast.4, bf16[1024,128]{1,0:T(8,128)(2,1)} %weight_h.1, f32[1,128]{1,0:T(1,128)} %bitcast.5, ...), custom_call_target="tpu_custom_call" | custom-call | tf_op jit(solution)/shard_map/whole/pallas_call | solution.py:325
  39.3 2.7 %tail.1 = (bf16[48,48,128]{2,1,0:T(8,128)(2,1)}, f32[1,12,32,128]{3,2,1,0:T(8,128)}, f32[1,12,32,128]{3,2,1,0:T(8,128)}, f32[1024,128]{1,0:T(8,128)}) custom-call(bf16[48,48,128]{2,1,0:T(8,128)(2,1)} %get-tuple-element.8.refs_0_, f32[1,12,32,128]{3,2,1,0:T(8,128)} %get-tuple-element.9.refs_1_, f32[1,12,32,128]{3,2,1,0:T(8,128)} %get-tuple-element.10.refs_2_, ...), custom_call_target="tpu_custom_call" | custom-call | tf_op jit(solution)/shard_map/tail/pallas_call | solution.py:373
where the time goes:
time: 42.1 us; the launch traced here: 42 us
  Pallas kernels  41.4 us (98%)
  between operations  0.64 us (2%)
    pallas_call x1, Pallas kernels, on_device(): pl.pallas_call(functools.partial(whole_kernel, n_row, n_col, 1.0 / n_s, 1...  38.7 us
    pallas_call x1, Pallas kernels, on_device(): pl.pallas_call(tail_kernel, out_shape=shapes, in_specs=[HBM] * 4, out_spe...  2.69 us

commit v1 on v0

--- a/solution.py
+++ b/solution.py
@@ -68,10 +68,9 @@
 def whole_kernel(
     n_row, n_col, inv_s, inv_w,
     left_h, right_h, weight_h, bias_h, grad_h,
-    out_p, out_l, out_r, out_w,
-    pair, sum_l, sum_r, left, right, weight, bias, grad,
+    pair, sum_l, sum_r, wide, left, right, weight, bias, grad,
     f_rows, f_w, a2, a2t, b2t, wp, wpt, xs, gs, gw_acc, gl_acc, gr_t,
-    gl, gr, gw, l_in, r_in, w_in, w_col, w_col_in, w_own, w_half,
+    gl, gr, gw, l_in, r_in, w_in, w_col, w_col_in, w_own, w_half, w_all,
     ls, lr, rs, rr, gls, glr, grs, grr, ws, wr, vs, vr, us, ur, ts, tr, loc,
 ):
     row, col = lax.axis_index("row"), lax.axis_index("col")
@@ -203,10 +202,10 @@
     def phase_4(hf, copies):
         for copy in copies:
             copy.wait()
-        mine = pltpu.make_async_copy(w_half.at[hf], out_w.at[hf, row], loc.at[7 + hf])
+        mine = pltpu.make_async_copy(w_half.at[hf], w_all.at[hf, row], loc.at[7 + hf])
         mine.start()
         return [mine] + spread(
-            lambda to: w_half.at[hf], out_w.at[hf, row], "row", n_row, row, ts.at[hf], tr.at[hf]
+            lambda to: w_half.at[hf], w_all.at[hf, row], "row", n_row, row, ts.at[hf], tr.at[hf]
         )
 
     lane = lax.broadcasted_iota(jnp.int32, (n_s, lanes), 1)
@@ -255,46 +254,31 @@
     pl.loop(0, early)(twice(update))
     w_b = phase_4(1, w_b)
     pl.loop(early, half // 4)(twice(update))
-    gives = [pltpu.make_async_copy(pair, out_p, loc.at[9])]
-    gives[0].start()
     for copy in c_l:
         copy.wait()
     total = gl[pl.ds(col * piece_l, piece_l)].astype(F32)
     for d in range(n_col - 1):
         total += l_in[d].astype(F32)
     sum_l[0] = total * inv_s
-    gives.append(pltpu.make_async_copy(sum_l, out_l, loc.at[10]))
-    gives[1].start()
     for copy in c_r:
         copy.wait()
     total = gr[pl.ds(row * piece_r, piece_r)].astype(F32)
     for d in range(n_row - 1):
         total += r_in[d].astype(F32)
     sum_r[0] = total * inv_s
-    gives.append(pltpu.make_async_copy(sum_r, out_r, loc.at[11]))
-    gives[2].start()
-    for copy in w_a + w_b + gives:
-        copy.wait()
+    for copy in w_a + w_b:
+        copy.wait()
+    flat = w_all[...].astype(F32).reshape(n_e, n_c, n_h)
+    for e in range(n_e):
+        f_w[:, e, :] = flat[e]
+    wide[...] = f_w[...].reshape(wide.shape)
 
 
 def tail_kernel(*refs):
-    inner, outer, held = refs[:4], refs[4:8], refs[8:12]
-    wide, mixed, arrived, left = refs[12:]
-    takes = [pltpu.make_async_copy(inner[at], held[at], arrived.at[at]) for at in range(4)]
-    gives = [
-        pltpu.make_async_copy(wide if at == 3 else held[at], outer[at], left.at[at]) for at in range(4)
-    ]
-    for at in (3, 0, 1, 2):
-        takes[at].start()
-    for at in (3, 0, 1, 2):
-        takes[at].wait()
-        if at == 3:
-            n_c, n_e, _ = mixed.shape
-            flat = held[3][...].astype(F32).reshape(wide.shape)
-            for e in range(n_e):
-                mixed[:, e, :] = flat[e * n_c : (e + 1) * n_c]
-            wide[...] = mixed[...].reshape(wide.shape)
-        gives[at].start()
+    inner, outer, sems = refs[:4], refs[4:8], refs[8]
+    gives = [pltpu.make_async_copy(src, dst, sems.at[at]) for at, (src, dst) in enumerate(zip(inner, outer))]
+    for copy in gives:
+        copy.start()
     for copy in gives:
         copy.wait()
 
@@ -321,14 +305,12 @@
         jax.ShapeDtypeStruct((1, piece_r, n_e, n_s), F32),
         jax.ShapeDtypeStruct((n_k, n_h), F32),
     )
-    held = shapes[:3] + (jax.ShapeDtypeStruct((2, n_row, n_col, small, n_h), BF),)
     results = pl.pallas_call(
         functools.partial(whole_kernel, n_row, n_col, 1.0 / n_s, 1.0 / (n_s * n_i * n_row)),
-        out_shape=held,
+        out_shape=tuple(pltpu.VMEM(shape.shape, shape.dtype) for shape in shapes),
         in_specs=[HBM] * 5,
-        out_specs=(HBM,) * 4,
-        scratch_shapes=[pltpu.VMEM(shape.shape, shape.dtype) for shape in held[:3]]
-        + [
+        out_specs=(VMEM,) * 4,
+        scratch_shapes=[
             pltpu.VMEM((n_col, piece_l, n_c, n_s), BF),
             pltpu.VMEM((n_row, piece_r, n_e, n_s), BF),
             pltpu.VMEM((n_k, n_h), BF),
@@ -356,6 +338,7 @@
             pltpu.VMEM((2, n_col - 1, small, n_h), BF),
             pltpu.VMEM((2, small, n_h), BF),
             pltpu.VMEM((2, n_col, small, n_h), BF),
+            pltpu.VMEM((2, n_row, n_col, small, n_h), BF),
         ]
         + [dma(n_col)] * 2
         + [dma(n_row)] * 2
@@ -364,20 +347,19 @@
         + [dma2(n_row)] * 2
         + [dma2(n_col)] * 4
         + [dma2(n_row)] * 2
-        + [dma(12)],
+        + [dma(9)],
         compiler_params=pltpu.CompilerParams(
-            collective_id=0, has_side_effects=True, vmem_limit_bytes=67043328 - 1536 * 1024
+            collective_id=0, has_side_effects=True, vmem_limit_bytes=56 * 1024 * 1024
         ),
         name="whole",
     )(left[0], right[0], weight, bias.reshape(1, n_h), grad)
     return pl.pallas_call(
         tail_kernel,
         out_shape=shapes,
-        in_specs=[HBM] * 4,
+        in_specs=[VMEM] * 4,
         out_specs=(HBM,) * 4,
-        scratch_shapes=[pltpu.VMEM(shape.shape, shape.dtype) for shape in held + shapes[3:]]
-        + [pltpu.VMEM((n_c, n_e, n_h), F32)]
-        + [dma(4), dma(4)],
+        scratch_shapes=[dma(4)],
+        compiler_params=pltpu.CompilerParams(vmem_limit_bytes=1024 * 1024),
         name="tail",
     )(*results)
 

time: 42.1 us -> 41 us (0.974)
  Pallas kernels: 41.4 us -> 40.2 us
    pallas_call x1, Pallas kernels: 2.69 us -> 1.15 us  [on_device(): pl.pallas_call(tail_kernel, out_shape=shapes, in_specs=[VMEM] * 4, out_sp...]
    pallas_call x1, Pallas kernels: 38.7 us -> 39.1 us  [on_device(): pl.pallas_call(functools.partial(whole_kernel, n_row, n_col, 1.0 / n_s, 1...]
where the time goes in v1:
time: 41 us; the launch traced here: 40.9 us
  Pallas kernels  40.2 us (98%)
  between operations  0.64 us (2%)
    pallas_call x1, Pallas kernels, on_device(): pl.pallas_call(functools.partial(whole_kernel, n_row, n_col, 1.0 / n_s, 1...  39.1 us
    pallas_call x1, Pallas kernels, on_device(): pl.pallas_call(tail_kernel, out_shape=shapes, in_specs=[VMEM] * 4, out_sp...  1.15 us

profile of v1, /device:TPU:0, one launch (start us, length us, event | category | flops | bytes accessed | tf_op | source)
XLA Modules:
  0.0 40.9 jit_solution(9304802059184033543)
XLA Ops:
  0.6 39.1 %whole.1 = (bf16[48,48,128]{2,1,0:T(8,128)(2,1)S(1)}, f32[1,12,32,128]{3,2,1,0:T(8,128)S(1)}, f32[1,12,32,128]{3,2,1,0:T(8,128)S(1)}, f32[1024,128]{1,0:T(8,128)S(1)}) custom-call(bf16[12,32,128]{2,1,0:T(8,128)(2,1)} %bitcast.3, bf16[12,32,128]{2,1,0:T(8,128)(2,1)} %bitcast.4, bf16[1024,128]{1,0:T(8,128)(2,1)} %weight_h.1, f32[1,128]{1,0:T(1,128)} %bitcast.5, ...), custom_call_target="tpu_custom_call" | custom-call | tf_op jit(solution)/shard_map/whole/pallas_call | solution.py:308
  39.7 1.2 %tail.1 = (bf16[48,48,128]{2,1,0:T(8,128)(2,1)}, f32[1,12,32,128]{3,2,1,0:T(8,128)}, f32[1,12,32,128]{3,2,1,0:T(8,128)}, f32[1024,128]{1,0:T(8,128)}) custom-call(bf16[48,48,128]{2,1,0:T(8,128)(2,1)S(1)} %get-tuple-element.8.refs_0_, f32[1,12,32,128]{3,2,1,0:T(8,128)S(1)} %get-tuple-element.9.refs_1_, f32[1,12,32,128]{3,2,1,0:T(8,128)S(1)} %get-tuple-element.10.refs_2_, ...), custom_call_target="tpu_custom_call" | custom-call | tf_op jit(solution)/shard_map/tail/pallas_call | solution.py:356

commit v2 on v1

v2 whole, which is shorter than its diff:
```python
import functools

import jax
import jax.numpy as jnp
from jax import lax
from jax.experimental import pallas as pl
from jax.experimental.pallas import tpu as pltpu
from jax.sharding import PartitionSpec as P

BF = jnp.bfloat16
F32 = jnp.float32
MESH = pl.DeviceIdType.MESH
VMEM = pl.BlockSpec(memory_space=pltpu.VMEM)
HBM = pl.BlockSpec(memory_space=pltpu.HBM)


def greet(n_row, n_col, row, col):
    barrier = pltpu.get_barrier_semaphore()
    for d in range(1, n_row):
        pl.semaphore_signal(barrier, inc=1, device_id={"row": lax.rem(row + d, n_row)}, device_id_type=MESH)
    for d in range(1, n_col):
        pl.semaphore_signal(barrier, inc=1, device_id={"col": lax.rem(col + d, n_col)}, device_id_type=MESH)
    pl.semaphore_wait(barrier, n_row + n_col - 2)


def send(src, dst, axis, to, send_sem, recv_sem):
    pltpu.make_async_remote_copy(
        src_ref=src, dst_ref=dst, send_sem=send_sem, recv_sem=recv_sem,
        device_id={axis: to}, device_id_type=MESH,
    ).start()


def fan(src_of, dst_of, axis, n, me, send_sem, recv_sem):
    for d in range(1, n):
        to = lax.rem(me + d, n)
        send(src_of(to), dst_of(d - 1), axis, to, send_sem, recv_sem)


def take(ref, sem):
    pltpu.make_async_copy(ref, ref, sem).wait()


def nn(a, b):
    return lax.dot_general(a, b, (((1,), (0,)), ((), ())), preferred_element_type=F32)


def nt(a, b):
    return lax.dot_general(a, b, (((1,), (1,)), ((), ())), preferred_element_type=F32)


def twice(body):
    def pair_of(p):
        body(p * 2)
        body(p * 2 + 1)

    return pair_of


def whole_kernel(
    n_row, n_col, inv_s, inv_w,
    left_h, right_h, weight_h, bias_h, grad_h,
    pair, sum_l, sum_r, wide, left, right, weight, bias, grad,
    f_rows, f_w, a2, a2t, b2t, wp, wpt, xs, gs, gw_acc, gl_acc, gr_t,
    gl, gr, gw, l_in, r_in, w_in, w_col, w_col_in, w_own, w_half, w_all,
    sent, l_got, got, w_sent, w_got, loc,
):
    row, col = lax.axis_index("row"), lax.axis_index("col")
    loads = [
        pltpu.make_async_copy(src, dst, loc.at[at])
        for at, (src, dst) in enumerate((
            (weight_h, weight), (grad_h, grad), (bias_h, bias),
            (right_h, right.at[row]), (left_h, left.at[col]),
        ))
    ]
    for copy in loads:
        copy.start()
    _, piece_l, n_c, n_s = left.shape
    _, piece_r, n_e, _ = right.shape
    n_i, n_j = n_col * piece_l, n_row * piece_r
    n_h = weight.shape[1]
    half, many = n_i // 2, piece_l
    pairs, step = n_col // 2, 4 if piece_l % 4 == 0 else piece_l
    pad = 64
    lanes = 2 * pad
    duo = lax.div(col, 2)
    greet(n_row, n_col, row, col)
    send(left_h, left.at[col], "col", col + 1 - 2 * lax.rem(col, 2), sent.at[0], l_got.at[0])
    fan(lambda to: right_h, lambda at: right.at[row], "row", n_row, row, sent.at[1], got.at[0])
    for g in range(1, pairs):
        for b in range(2):
            to = 2 * lax.rem(duo + g, pairs) + b
            send(left_h, left.at[col], "col", to, sent.at[0], l_got.at[pairs - g])

    loads[0].wait()
    f_w[...] = weight[...].astype(F32).reshape(n_c, n_e, n_h)
    for e in range(n_e):
        wp[e * n_c : (e + 1) * n_c, :] = f_w[:, e, :].astype(BF)
    wpt[...] = wp[...].T
    loads[1].wait()
    loads[2].wait()
    zeros = jnp.zeros((pad - n_j, n_h), BF)

    def low(ip):
        return ip + lax.div(ip, many) * many

    def grads(ip, count):
        rows = []
        for q in range(count):
            at = low(ip + q)
            rows += [grad[at], zeros, grad[at + many], zeros]
        return jnp.concatenate(rows, axis=0)

    @pl.loop(0, half // 2)
    def _(p):
        ip = p * 2
        og = nt(wp[...], grads(ip, 2)).astype(BF)
        for q in range(2):
            gs[ip + q] = og[:, q * lanes : (q + 1) * lanes].reshape(n_e, n_c, lanes)

    b2t[...] = jnp.zeros_like(b2t)
    gw_acc[...] = jnp.zeros_like(gw_acc)
    gl_acc[...] = jnp.zeros_like(gl_acc)
    loads[3].wait()
    take(right.at[pl.ds(0, n_row - 1)], got.at[0])
    f_rows[...] = right[...].reshape(n_j, n_e, n_s).astype(F32)
    for e in range(n_e):
        block = f_rows[:, e, :].astype(BF)
        b2t[e, 0:n_j, 0:n_s] = block
        b2t[e, pad : pad + n_j, n_s : 2 * n_s] = block

    width = n_e // 2

    def means(ip, count, first, size):
        return jnp.concatenate(
            [xs[ip + q, first : first + size].reshape(size * n_c, lanes) for q in range(count)], axis=1
        )

    def base_of(g):
        return lax.rem(duo + g, pairs) * many

    def arrive(g):
        at = lax.rem(duo + g, pairs)
        if g == 0:
            loads[4].wait()
            take(left.at[0], l_got.at[0])
        else:
            take(left.at[pl.ds(0, 2)], l_got.at[g])
        for ii in range(2):
            block = left[at * 2 + ii].reshape(many * n_c, n_s)
            a2[pl.ds(at * many * n_c, many * n_c), ii * n_s : (ii + 1) * n_s] = block

    def terms(g, hf):
        base, first = base_of(g), hf * width

        @pl.loop(0, width // 8)
        def _(p):
            rows = a2[pl.ds(base * n_c, many * n_c)]
            for k in range(4):
                e = first + p * 8 + 2 * k
                out = nt(rows, b2t[pl.ds(e, 2)].reshape(2 * lanes, 2 * n_s)).astype(BF)
                for q in range(2):
                    xs[pl.ds(base, many), pl.ds(e + q, 1)] = out[:, q * lanes : (q + 1) * lanes].reshape(
                        many, 1, n_c, lanes
                    )

        @pl.loop(0, many // step)
        def _(p):
            ip = base + p * step
            gw_acc[hf] += nn(means(ip, step, first, width), grads(ip, step))

    def phase_1(hf):
        gw[hf] = gw_acc[hf].reshape(gw.shape[1:]).astype(BF)
        fan(
            lambda to: gw.at[hf, to], lambda at: w_in.at[hf, at], "row", n_row, row,
            w_sent.at[hf], w_got.at[hf],
        )

    def phase_2(hf):
        take(w_in.at[hf], w_got.at[hf])
        total = gw[hf, row].astype(F32)
        for d in range(n_row - 1):
            total += w_in[hf, d].astype(F32)
        w_col[hf] = total.reshape(w_col.shape[1:]).astype(BF)
        fan(
            lambda to: w_col.at[hf, to], lambda at: w_col_in.at[hf, at], "col", n_col, col,
            w_sent.at[2 + hf], w_got.at[2 + hf],
        )

    def phase_3(hf):
        take(w_col_in.at[hf], w_got.at[2 + hf])
        total = w_col[hf, col].astype(F32)
        for d in range(n_col - 1):
            total += w_col_in[hf, d].astype(F32)
        w_own[hf] = (total * inv_w).astype(BF)
        fan(
            lambda to: w_own.at[hf], lambda at: w_half.at[hf, col], "col", n_col, col,
            w_sent.at[4 + hf], w_got.at[4 + hf],
        )
        mine = pltpu.make_async_copy(w_own.at[hf], w_half.at[hf, col], loc.at[5 + hf])
        mine.start()
        return mine

    def phase_4(hf, mine):
        mine.wait()
        take(w_half.at[hf, pl.ds(0, n_col - 1)], w_got.at[4 + hf])
        fan(
            lambda to: w_half.at[hf], lambda at: w_all.at[hf, row], "row", n_row, row,
            w_sent.at[6 + hf], w_got.at[6 + hf],
        )
        mine = pltpu.make_async_copy(w_half.at[hf], w_all.at[hf, row], loc.at[7 + hf])
        mine.start()
        return mine

    def finish(hf, mine):
        mine.wait()
        take(w_all.at[hf, pl.ds(0, n_row - 1)], w_got.at[6 + hf])
        flat = w_all[hf].reshape(width, n_c, n_h)
        for e in range(width):
            wide[:, hf * width + e, :] = flat[e].astype(F32)

    def lefts(p):
        e = p * 4
        g = jnp.concatenate([gs[:, e + q].reshape(half * n_c, lanes) for q in range(4)], axis=1)
        gl_acc[...] += nn(g, b2t[pl.ds(e, 4)].reshape(4 * lanes, 2 * n_s))

    lane = lax.broadcasted_iota(jnp.int32, (n_s, lanes), 1)

    def rights(p):
        e = p * 2
        g = jnp.concatenate([gs[:, e + q].reshape(half * n_c, lanes) for q in range(2)], axis=1)
        t = nn(a2t[...], g)
        for q in range(2):
            z = jnp.where(
                lane < pad,
                t[0:n_s, q * lanes : (q + 1) * lanes],
                t[n_s : 2 * n_s, q * lanes : (q + 1) * lanes],
            ).T
            gr_t[e + q] = z[0:n_j] + z[pad : pad + n_j]

    def give_right(hf):
        for e in range(hf * width, (hf + 1) * width):
            f_rows[:, e, :] = gr_t[e]
        gr[hf] = f_rows[:, hf * width : (hf + 1) * width, :].astype(BF)
        fan(
            lambda to: gr.at[hf, pl.ds(to * piece_r, piece_r)], lambda at: r_in.at[hf, at], "row", n_row, row,
            sent.at[3 + hf], got.at[2 + hf],
        )

    def update(p):
        ip = p * 2
        up = nn(wpt[...], means(ip, 2, 0, n_e))
        for q in range(2):
            u = (up[:, q * lanes : (q + 1) * lanes].T * inv_s + bias[...]).astype(BF)
            at = low(ip + q)
            pair[at] = u[0:n_j]
            pair[at + many] = u[pad : pad + n_j]

    for g in range(pairs):
        arrive(g)
        if g < pairs - 1:
            terms(g, 0)
            terms(g, 1)
    terms(pairs - 1, 0)
    phase_1(0)
    terms(pairs - 1, 1)
    phase_1(1)
    a2t[...] = a2[...].T
    quarter = n_e // 8
    pl.loop(0, quarter)(lefts)
    phase_2(0)
    pl.loop(quarter, 2 * quarter)(lefts)
    phase_2(1)
    for ii in range(2):
        gl[:, ii] = gl_acc[:, ii * n_s : (ii + 1) * n_s].reshape(pairs, many, n_c, n_s).astype(BF)
    fan(lambda to: gl.at[lax.div(to, 2), lax.rem(to, 2)], lambda at: l_in.at[at], "col", n_col, col, sent.at[2], got.at[1])
    pl.loop(0, width // 4)(twice(rights))
    w_a = phase_3(0)
    give_right(0)
    pl.loop(width // 4, width // 2)(twice(rights))
    w_b = phase_3(1)
    give_right(1)
    early = half // 12
    pl.loop(0, early)(twice(update))
    w_a = phase_4(0, w_a)
    pl.loop(early, half // 4)(twice(update))
    w_b = phase_4(1, w_b)
    take(l_in, got.at[1])
    total = gl[duo, lax.rem(col, 2)].astype(F32)
    for d in range(n_col - 1):
        total += l_in[d].astype(F32)
    sum_l[0] = total * inv_s
    finish(0, w_a)
    for hf in range(2):
        take(r_in.at[hf], got.at[2 + hf])
        total = gr[hf, pl.ds(row * piece_r, piece_r)].astype(F32)
        for d in range(n_row - 1):
            total += r_in[hf, d].astype(F32)
        sum_r[0, :, hf * width : (hf + 1) * width, :] = total * inv_s
    finish(1, w_b)
    take(left.at[pl.ds(0, n_col - 1)], sent.at[0])
    take(right.at[pl.ds(0, n_row - 1)], sent.at[1])
    take(l_in, sent.at[2])
    for hf in range(2):
        take(r_in.at[hf], sent.at[3 + hf])
        take(w_in.at[hf], w_sent.at[hf])
        take(w_col_in.at[hf], w_sent.at[2 + hf])
        take(w_half.at[hf, pl.ds(0, n_col - 1)], w_sent.at[4 + hf])
        take(w_all.at[hf, pl.ds(0, n_row - 1)], w_sent.at[6 + hf])


def tail_kernel(*refs):
    inner, outer, sems = refs[:4], refs[4:8], refs[8]
    gives = [pltpu.make_async_copy(src, dst, sems.at[at]) for at, (src, dst) in enumerate(zip(inner, outer))]
    for copy in gives:
        copy.start()
    for copy in gives:
        copy.wait()


def dma(n):
    return pltpu.SemaphoreType.DMA((n,))


def on_device(n_row, n_col, left, right, weight, bias, grad):
    _, piece_l, n_c, n_s = left.shape
    _, piece_r, n_e, _ = right.shape
    n_k, n_h = weight.shape
    n_i, n_j = piece_l * n_col, piece_r * n_row
    half, lanes = n_i // 2, 128
    part = n_k // 2 // n_row
    small = part // n_col
    shapes = (
        jax.ShapeDtypeStruct((n_i, n_j, n_h), BF),
        jax.ShapeDtypeStruct((1, piece_l, n_c, n_s), F32),
        jax.ShapeDtypeStruct((1, piece_r, n_e, n_s), F32),
        jax.ShapeDtypeStruct((n_c, n_e, n_h), F32),
    )
    results = pl.pallas_call(
        functools.partial(whole_kernel, n_row, n_col, 1.0 / n_s, 1.0 / (n_s * n_i * n_row)),
        out_shape=tuple(pltpu.VMEM(shape.shape, shape.dtype) for shape in shapes),
        in_specs=[HBM] * 5,
        out_specs=(VMEM,) * 4,
        scratch_shapes=[
            pltpu.VMEM((n_col, piece_l, n_c, n_s), BF),
            pltpu.VMEM((n_row, piece_r, n_e, n_s), BF),
            pltpu.VMEM((n_k, n_h), BF),
            pltpu.VMEM((1, n_h), F32),
            pltpu.VMEM((n_i, n_j, n_h), BF),
            pltpu.VMEM((n_j, n_e, n_s), F32),
            pltpu.VMEM((n_c, n_e, n_h), F32),
            pltpu.VMEM((half * n_c, 2 * n_s), BF),
            pltpu.VMEM((2 * n_s, half * n_c), BF),
            pltpu.VMEM((n_e, lanes, 2 * n_s), BF),
            pltpu.VMEM((n_k, n_h), BF),
            pltpu.VMEM((n_h, n_k), BF),
            pltpu.VMEM((half, n_e, n_c, lanes), BF),
            pltpu.VMEM((half, n_e, n_c, lanes), BF),
            pltpu.VMEM((2, n_k // 2, n_h), F32),
            pltpu.VMEM((half * n_c, 2 * n_s), F32),
            pltpu.VMEM((n_e, n_j, n_s), F32),
            pltpu.VMEM((n_col // 2, 2, piece_l, n_c, n_s), BF),
            pltpu.VMEM((2, n_j, n_e // 2, n_s), BF),
            pltpu.VMEM((2, n_row, part, n_h), BF),
            pltpu.VMEM((n_col - 1, piece_l, n_c, n_s), BF),
            pltpu.VMEM((2, n_row - 1, piece_r, n_e // 2, n_s), BF),
            pltpu.VMEM((2, n_row - 1, part, n_h), BF),
            pltpu.VMEM((2, n_col, small, n_h), BF),
            pltpu.VMEM((2, n_col - 1, small, n_h), BF),
            pltpu.VMEM((2, small, n_h), BF),
            pltpu.VMEM((2, n_col, small, n_h), BF),
            pltpu.VMEM((2, n_row, n_col, small, n_h), BF),
        ]
        + [dma(5), dma(n_col // 2), dma(4), dma(8), dma(8), dma(9)],
        compiler_params=pltpu.CompilerParams(
            collective_id=0, has_side_effects=True, vmem_limit_bytes=56 * 1024 * 1024
        ),
        name="whole",
    )(left[0], right[0], weight, bias.reshape(1, n_h), grad)
    out_p, out_l, out_r, out_w = pl.pallas_call(
        tail_kernel,
        out_shape=shapes,
        in_specs=[VMEM] * 4,
        out_specs=(HBM,) * 4,
        scratch_shapes=[dma(4)],
        compiler_params=pltpu.CompilerParams(vmem_limit_bytes=1024 * 1024),
        name="tail",
    )(*results)
    return out_p, out_l, out_r, out_w.reshape(n_k, n_h)


def solution(mesh):
    return jax.shard_map(
        functools.partial(on_device, mesh.shape["row"], mesh.shape["col"]),
        mesh=mesh,
        in_specs=(
            P(("grp", "row"), "col", None, None),
            P(("grp", "col"), "row", None, None),
            P(),
            P(),
            P(("grp", "row"), "col", None),
        ),
        out_specs=(
            P(("grp", "row"), "col", None),
            P(("grp", "row"), "col", None, None),
            P(("grp", "col"), "row", None, None),
            P("grp", None),
        ),
        check_vma=False,
    )
```

time: 41 us -> 41.4 us (level)
  no operation moved by 1% of the time
where the time goes in v2:
time: 41.4 us; the launch traced here: 41.3 us
  Pallas kernels  40.6 us (98%)
  between operations  0.64 us (2%)
    pallas_call x1, Pallas kernels, on_device(): pl.pallas_call(functools.partial(whole_kernel, n_row, n_col, 1.0 / n_s, 1...  39.5 us
    pallas_call x1, Pallas kernels, on_device(): pl.pallas_call(tail_kernel, out_shape=shapes, in_specs=[VMEM] * 4, out_sp...  1.15 us

profile of v2, /device:TPU:0, one launch (start us, length us, event | category | flops | bytes accessed | tf_op | source)
XLA Modules:
  0.0 41.3 jit_solution(16227914898976968007)
XLA Ops:
  0.6 39.5 %whole.1 = (bf16[48,48,128]{2,1,0:T(8,128)(2,1)S(1)}, f32[1,12,32,128]{3,2,1,0:T(8,128)S(1)}, f32[1,12,32,128]{3,2,1,0:T(8,128)S(1)}, f32[32,32,128]{2,1,0:T(8,128)S(1)}) custom-call(bf16[12,32,128]{2,1,0:T(8,128)(2,1)} %bitcast.4, bf16[12,32,128]{2,1,0:T(8,128)(2,1)} %bitcast.5, bf16[1024,128]{1,0:T(8,128)(2,1)} %weight_h.1, f32[1,128]{1,0:T(1,128)} %bitcast.6, ...), custom_call_target="tpu_custom_call" | custom-call | tf_op jit(solution)/shard_map/whole/pallas_call | solution.py:338
  40.1 1.2 %tail.1 = (bf16[48,48,128]{2,1,0:T(8,128)(2,1)}, f32[1,12,32,128]{3,2,1,0:T(8,128)}, f32[1,12,32,128]{3,2,1,0:T(8,128)}, f32[32,32,128]{2,1,0:T(8,128)}) custom-call(bf16[48,48,128]{2,1,0:T(8,128)(2,1)S(1)} %get-tuple-element.12.refs_0_, f32[1,12,32,128]{3,2,1,0:T(8,128)S(1)} %get-tuple-element.13.refs_1_, f32[1,12,32,128]{3,2,1,0:T(8,128)S(1)} %get-tuple-element.14.refs_2_, ...), custom_call_target="tpu_custom_call" | custom-call | tf_op jit(solution)/shard_map/tail/pallas_call | solution.py:379

commit v3 on v2

--- a/solution.py
+++ b/solution.py
@@ -255,6 +255,25 @@
             pair[at] = u[0:n_j]
             pair[at + many] = u[pad : pad + n_j]
 
+    def trickle(t):
+        part = pl.ds(t, 1)
+        fan(
+            lambda to: gl.at[lax.div(to, 2), lax.rem(to, 2), part], lambda at: l_in.at[at, part],
+            "col", n_col, col, sent.at[2], got.at[1],
+        )
+
+    def trickling(body, start):
+        def trip(p):
+            if piece_l < width // 2 + 2 * early:
+                pl.when(start + p < piece_l)(lambda: trickle(start + p))
+            else:
+                trickle(start + p)
+            body(p * 2)
+            body(p * 2 + 1)
+
+        return trip
+
+    early = half // 12
     for g in range(pairs):
         arrive(g)
         if g < pairs - 1:
@@ -272,17 +291,18 @@
     phase_2(1)
     for ii in range(2):
         gl[:, ii] = gl_acc[:, ii * n_s : (ii + 1) * n_s].reshape(pairs, many, n_c, n_s).astype(BF)
-    fan(lambda to: gl.at[lax.div(to, 2), lax.rem(to, 2)], lambda at: l_in.at[at], "col", n_col, col, sent.at[2], got.at[1])
-    pl.loop(0, width // 4)(twice(rights))
+    pl.loop(0, width // 4)(trickling(rights, 0))
     w_a = phase_3(0)
     give_right(0)
-    pl.loop(width // 4, width // 2)(twice(rights))
+    pl.loop(width // 4, width // 2)(trickling(rights, 0))
     w_b = phase_3(1)
     give_right(1)
-    early = half // 12
-    pl.loop(0, early)(twice(update))
+    pl.loop(0, early)(trickling(update, width // 2))
     w_a = phase_4(0, w_a)
-    pl.loop(early, half // 4)(twice(update))
+    pl.loop(early, 2 * early)(trickling(update, width // 2))
+    pl.loop(2 * early, half // 4)(twice(update))
+    for t in range(width // 2 + 2 * early, piece_l):
+        trickle(t)
     w_b = phase_4(1, w_b)
     take(l_in, got.at[1])
     total = gl[duo, lax.rem(col, 2)].astype(F32)

time: 41.4 us -> 38.4 us (0.928)
  Pallas kernels: 40.6 us -> 37.6 us
    pallas_call x1, Pallas kernels: 39.5 us -> 36.4 us  [on_device(): pl.pallas_call(functools.partial(whole_kernel, n_row, n_col, 1.0 / n_s, 1...]
where the time goes in v3:
time: 38.4 us; the launch traced here: 38.2 us
  Pallas kernels  37.6 us (98%)
  between operations  0.64 us (2%)
    pallas_call x1, Pallas kernels, on_device(): pl.pallas_call(functools.partial(whole_kernel, n_row, n_col, 1.0 / n_s, 1...  36.4 us
    pallas_call x1, Pallas kernels, on_device(): pl.pallas_call(tail_kernel, out_shape=shapes, in_specs=[VMEM] * 4, out_sp...  1.15 us

profile of v3, /device:TPU:0, one launch (start us, length us, event | category | flops | bytes accessed | tf_op | source)
XLA Modules:
  0.0 38.2 jit_solution(7283206494213684001)
XLA Ops:
  0.6 36.4 %whole.1 = (bf16[48,48,128]{2,1,0:T(8,128)(2,1)S(1)}, f32[1,12,32,128]{3,2,1,0:T(8,128)S(1)}, f32[1,12,32,128]{3,2,1,0:T(8,128)S(1)}, f32[32,32,128]{2,1,0:T(8,128)S(1)}) custom-call(bf16[12,32,128]{2,1,0:T(8,128)(2,1)} %bitcast.4, bf16[12,32,128]{2,1,0:T(8,128)(2,1)} %bitcast.5, bf16[1024,128]{1,0:T(8,128)(2,1)} %weight_h.1, f32[1,128]{1,0:T(1,128)} %bitcast.6, ...), custom_call_target="tpu_custom_call" | custom-call | tf_op jit(solution)/shard_map/whole/pallas_call | solution.py:358
  37.1 1.2 %tail.1 = (bf16[48,48,128]{2,1,0:T(8,128)(2,1)}, f32[1,12,32,128]{3,2,1,0:T(8,128)}, f32[1,12,32,128]{3,2,1,0:T(8,128)}, f32[32,32,128]{2,1,0:T(8,128)}) custom-call(bf16[48,48,128]{2,1,0:T(8,128)(2,1)S(1)} %get-tuple-element.12.refs_0_, f32[1,12,32,128]{3,2,1,0:T(8,128)S(1)} %get-tuple-element.13.refs_1_, f32[1,12,32,128]{3,2,1,0:T(8,128)S(1)} %get-tuple-element.14.refs_2_, ...), custom_call_target="tpu_custom_call" | custom-call | tf_op jit(solution)/shard_map/tail/pallas_call | solution.py:399
